TPU v7x, 32 devices: a whole 2x2x4 slice. The times are simulated.
32 devices in a mesh: dp: 4 (over y, x), seq: 8 (over z, core).
Axes of the slice: x: 2, y: 2, z: 4, core: 2. Of those that a mesh axis runs over, the one named last changes fastest.
Arguments:
- inputs: bfloat16 [8, 1024, 1280], P('dp', 'seq'), may hold values from -6 to 6
- cotangent: bfloat16 [8, 1024, 1280], P('dp', 'seq'), may hold values from -6 to 6
- w_query: bfloat16 [1280, 1280], P(('dp', 'seq')), may hold values from -0.15625 to 0.15625
- w_key: bfloat16 [1280, 1280], P(('dp', 'seq')), may hold values from -0.15625 to 0.15625
- w_value: bfloat16 [1280, 1280], P(('dp', 'seq')), may hold values from -0.15625 to 0.15625
- w_out: bfloat16 [1280, 1280], P(('dp', 'seq')), may hold values from -1.25 to 1.25
- w_up: bfloat16 [1280, 1280], P(('dp', 'seq')), may hold values from -0.15625 to 0.15625
- w_down: bfloat16 [1280, 1280], P(('dp', 'seq')), may hold values from -0.15625 to 0.15625
- norm_attn: bfloat16 [1280], P(('dp', 'seq')), may hold values from 0.5 to 1.5
- norm_mlp: bfloat16 [1280], P(('dp', 'seq')), may hold values from 0.5 to 1.5
- query_scale: bfloat16 [1280], P(('dp', 'seq')), may hold values from 0 to 1.5
Outputs:
- output: bfloat16 [8, 1024, 1280], P('dp', 'seq')
- input_grad: float32 [8, 1024, 1280], P('dp', 'seq')
- grad_query: float32 [1280, 1280], P(('dp', 'seq'))
- grad_key: float32 [1280, 1280], P(('dp', 'seq'))
- grad_value: float32 [1280, 1280], P(('dp', 'seq'))
- grad_out: float32 [1280, 1280], P(('dp', 'seq'))
- grad_up: float32 [1280, 1280], P(('dp', 'seq'))
- grad_down: float32 [1280, 1280], P(('dp', 'seq'))
- grad_norm_attn: float32 [1280], P(('dp', 'seq'))
- grad_norm_mlp: float32 [1280], P(('dp', 'seq'))
- grad_query_scale: float32 [1280], P(('dp', 'seq'))
All inputs are finite; a program needn't handle non-finite values.
Results may differ from a plain program's by a relative error of at most 0.014.
Values may be sent and summed in bfloat16 or wider, within the bound.
No kernel may reach another device: no remote copies, remote signals or barrier semaphores. Data moves between devices by JAX's collectives and lax.ppermute only.
A program may use at most 320 MiB of HBM per device.

v0:
```python
import math
import jax
import jax.numpy as jnp
from jax import lax
from jax.sharding import PartitionSpec as P

H = 16
EPS = 1e-06
SOFT_BASE = 1.442695


def weight_outer(left, right):
    return lax.dot_general(
        left, right, (((0,), (0,)), ((), ())), preferred_element_type=jnp.float32
    )


def times_transpose(left, right):
    return lax.dot_general(
        left, right, (((1,), (1,)), ((), ())), preferred_element_type=jnp.float32
    )


def norm_back(grad, normed, inverse, gain):
    scaled = grad * gain
    inner = jnp.mean(scaled * normed, axis=-1, keepdims=True)
    return (inverse * (scaled - normed * inner), jnp.sum(grad * normed, axis=0))


def attend(q_low, k_low, v_low, first_row, num_heads):
    group_rows, model_width = q_low.shape
    head_size = model_width // num_heads
    query_heads = q_low.reshape(group_rows, num_heads, head_size)
    query_place = first_row + lax.iota(jnp.int32, group_rows)
    start_state = (
        jnp.full((num_heads, group_rows), -1e30, jnp.float32),
        jnp.zeros((num_heads, group_rows), jnp.float32),
        jnp.zeros((group_rows, model_width), jnp.float32),
    )
    key_piece = lax.all_gather(k_low, "seq", axis=0, tiled=True)
    value_piece = lax.all_gather(v_low, "seq", axis=0, tiled=True)
    count = key_piece.shape[0]

    def attend_compute(state):
        best, total, accum = state
        key_heads = key_piece.reshape(count, num_heads, head_size)
        value_heads = value_piece.reshape(count, num_heads, head_size)
        scores = jnp.einsum(
            "qhd,khd->hqk", query_heads, key_heads, preferred_element_type=jnp.float32
        )
        key_place = lax.iota(jnp.int32, count)
        allowed = (key_place[None, :] <= query_place[:, None])[None]
        scores = jnp.where(allowed, scores, -1e30)
        fresh = jnp.maximum(best, jnp.max(scores, axis=2))
        shrink = jnp.exp(best - fresh)
        probs = jnp.where(allowed, jnp.exp(scores - fresh[:, :, None]), 0.0)
        total = jnp.sum(probs, axis=2)
        mixed = jnp.einsum(
            "hqk,khd->qhd",
            probs.astype(jnp.bfloat16),
            value_heads,
            preferred_element_type=jnp.float32,
        )
        factor = jnp.repeat(shrink.T, head_size, axis=1)
        return (fresh, total, accum * factor + mixed.reshape(group_rows, model_width))

    best, total, accum = lax.cond(
        jnp.int32(0) > first_row + group_rows - 1, lambda state: state, attend_compute, start_state
    )
    mixed = accum / jnp.repeat(total.T, head_size, axis=1)
    return (mixed, best + jnp.log(total))


def query_grads(q_low, d_mixed, k_low, v_low, log_total, row_delta, first_row, num_heads):
    group_rows, model_width = q_low.shape
    head_size = model_width // num_heads
    query_heads = q_low.reshape(group_rows, num_heads, head_size)
    grad_heads = d_mixed.reshape(group_rows, num_heads, head_size)
    query_place = first_row + lax.iota(jnp.int32, group_rows)
    empty = jnp.zeros((group_rows, model_width), jnp.float32)
    key_piece = lax.all_gather(k_low, "seq", axis=0, tiled=True)
    value_piece = lax.all_gather(v_low, "seq", axis=0, tiled=True)
    count = key_piece.shape[0]

    def query_compute(accum):
        key_heads = key_piece.reshape(count, num_heads, head_size)
        value_heads = value_piece.reshape(count, num_heads, head_size)
        scores = jnp.einsum(
            "qhd,khd->hqk", query_heads, key_heads, preferred_element_type=jnp.float32
        )
        key_place = lax.iota(jnp.int32, count)
        allowed = (key_place[None, :] <= query_place[:, None])[None]
        probs = jnp.where(allowed, jnp.exp(scores - log_total[:, :, None]), 0.0)
        d_prob = jnp.einsum(
            "qhd,khd->hqk", grad_heads, value_heads, preferred_element_type=jnp.float32
        )
        d_score = (probs * (d_prob - row_delta[:, :, None])).astype(jnp.bfloat16)
        added = jnp.einsum("hqk,khd->qhd", d_score, key_heads, preferred_element_type=jnp.float32)
        return added.reshape(group_rows, model_width)

    return lax.cond(
        jnp.int32(0) > first_row + group_rows - 1, lambda accum: accum, query_compute, empty
    )


def key_grads(k_low, v_low, q_low, d_mixed, total_all, delta_all, first_row, num_heads):
    group_rows, model_width = k_low.shape
    head_size = model_width // num_heads
    key_heads = k_low.reshape(group_rows, num_heads, head_size)
    value_heads = v_low.reshape(group_rows, num_heads, head_size)
    key_place = first_row + lax.iota(jnp.int32, group_rows)
    empty = jnp.zeros((group_rows, model_width), jnp.float32)
    query_piece = lax.all_gather(q_low, "seq", axis=0, tiled=True)
    grad_piece = lax.all_gather(d_mixed, "seq", axis=0, tiled=True)
    count = query_piece.shape[0]

    def key_compute(state):
        query_heads = query_piece.reshape(count, num_heads, head_size)
        grad_heads = grad_piece.reshape(count, num_heads, head_size)
        scores = jnp.einsum(
            "qhd,khd->hqk", query_heads, key_heads, preferred_element_type=jnp.float32
        )
        query_place = lax.iota(jnp.int32, count)
        allowed = (key_place[None, :] <= query_place[:, None])[None]
        probs = jnp.where(allowed, jnp.exp(scores - total_all[:, :, None]), 0.0)
        d_prob = jnp.einsum(
            "qhd,khd->hqk", grad_heads, value_heads, preferred_element_type=jnp.float32
        )
        d_score = (probs * (d_prob - delta_all[:, :, None])).astype(jnp.bfloat16)
        more_values = jnp.einsum(
            "hqk,qhd->khd",
            probs.astype(jnp.bfloat16),
            grad_heads,
            preferred_element_type=jnp.float32,
        )
        more_keys = jnp.einsum(
            "hqk,qhd->khd", d_score, query_heads, preferred_element_type=jnp.float32
        )
        return (
            more_keys.reshape(group_rows, model_width),
            more_values.reshape(group_rows, model_width),
        )

    return lax.cond(
        jnp.int32(0) + count - 1 < first_row, lambda state: state, key_compute, (empty, empty)
    )


def per_device(
    inputs,
    cotangent,
    w_query,
    w_key,
    w_value,
    w_out,
    w_up,
    w_down,
    norm_attn,
    norm_mlp,
    query_scale,
):
    micro_count, group_rows, model_width = inputs.shape
    num_heads = H
    head_size = model_width // num_heads
    first_row = lax.axis_index("seq") * group_rows
    results = []
    in_grads = []
    totals = None
    for micro_index in range(micro_count):
        gathered = (
            lax.all_gather(w_query, ("dp", "seq"), axis=0, tiled=True),
            lax.all_gather(w_key, ("dp", "seq"), axis=0, tiled=True),
            lax.all_gather(w_value, ("dp", "seq"), axis=0, tiled=True),
            lax.all_gather(w_out, ("dp", "seq"), axis=0, tiled=True),
            lax.all_gather(w_up, ("dp", "seq"), axis=0, tiled=True),
            lax.all_gather(w_down, ("dp", "seq"), axis=0, tiled=True),
            lax.all_gather(norm_attn, ("dp", "seq"), axis=0, tiled=True),
            lax.all_gather(norm_mlp, ("dp", "seq"), axis=0, tiled=True),
            lax.all_gather(query_scale, ("dp", "seq"), axis=0, tiled=True),
        )
        full_query, full_key, full_value, full_out, full_up, full_down = gathered[:6]
        gain_attn = gathered[6].astype(jnp.float32)
        gain_mlp = gathered[7].astype(jnp.float32)
        scale_param = gathered[8].astype(jnp.float32)
        scale = jax.nn.softplus(scale_param) * (SOFT_BASE / math.sqrt(head_size))
        layer_in = inputs[micro_index].astype(jnp.float32)
        inv_attn = lax.rsqrt(jnp.mean(layer_in * layer_in, axis=-1, keepdims=True) + EPS)
        normed_attn = layer_in * inv_attn
        h_attn = (normed_attn * gain_attn).astype(jnp.bfloat16)
        q_raw = jnp.dot(h_attn, full_query, preferred_element_type=jnp.float32)
        q_low = (q_raw * scale).astype(jnp.bfloat16)
        k_low = jnp.dot(h_attn, full_key, preferred_element_type=jnp.float32).astype(jnp.bfloat16)
        v_low = jnp.dot(h_attn, full_value, preferred_element_type=jnp.float32).astype(jnp.bfloat16)
        mixed, log_total = attend(q_low, k_low, v_low, first_row, num_heads)
        attn_in = mixed.astype(jnp.bfloat16)
        resid = layer_in + jnp.dot(attn_in, full_out, preferred_element_type=jnp.float32)
        inv_mlp = lax.rsqrt(jnp.mean(resid * resid, axis=-1, keepdims=True) + EPS)
        normed_mlp = resid * inv_mlp
        h_mlp = (normed_mlp * gain_mlp).astype(jnp.bfloat16)
        up_proj = jnp.dot(h_mlp, full_up, preferred_element_type=jnp.float32)
        activated = jax.nn.silu(up_proj).astype(jnp.bfloat16)
        layer_out = resid + jnp.dot(activated, full_down, preferred_element_type=jnp.float32)
        results.append(layer_out.astype(jnp.bfloat16))
        regathered = (
            lax.all_gather(w_query, ("dp", "seq"), axis=0, tiled=True),
            lax.all_gather(w_key, ("dp", "seq"), axis=0, tiled=True),
            lax.all_gather(w_value, ("dp", "seq"), axis=0, tiled=True),
            lax.all_gather(w_out, ("dp", "seq"), axis=0, tiled=True),
            lax.all_gather(w_up, ("dp", "seq"), axis=0, tiled=True),
            lax.all_gather(w_down, ("dp", "seq"), axis=0, tiled=True),
        )
        back_query, back_key, back_value, back_out, back_up, back_down = regathered
        cotan_rows = cotangent[micro_index]
        cotan_float = cotan_rows.astype(jnp.float32)
        grad_down = weight_outer(activated, cotan_rows)
        d_act = times_transpose(cotan_rows, back_down)
        sigmoid_up = jax.nn.sigmoid(up_proj)
        d_up = (d_act * sigmoid_up * (1.0 + up_proj * (1.0 - sigmoid_up))).astype(jnp.bfloat16)
        grad_up = weight_outer(h_mlp, d_up)
        d_hmlp = times_transpose(d_up, back_up)
        d_norm_mlp, grad_gain_mlp = norm_back(d_hmlp, normed_mlp, inv_mlp, gain_mlp)
        d_resid = cotan_float + d_norm_mlp
        resid_low = d_resid.astype(jnp.bfloat16)
        grad_out = weight_outer(attn_in, resid_low)
        d_mixed = times_transpose(resid_low, back_out).astype(jnp.bfloat16)
        row_delta = jnp.sum(
            (d_mixed.astype(jnp.float32) * mixed).reshape(group_rows, num_heads, head_size), axis=2
        ).T
        total_all, delta_all = (
            lax.all_gather(log_total, "seq", axis=1, tiled=True),
            lax.all_gather(row_delta, "seq", axis=1, tiled=True),
        )
        d_qlow = query_grads(
            q_low, d_mixed, k_low, v_low, log_total, row_delta, first_row, num_heads
        )
        d_keys, d_values = key_grads(
            k_low, v_low, q_low, d_mixed, total_all, delta_all, first_row, num_heads
        )
        keys_low = d_keys.astype(jnp.bfloat16)
        values_low = d_values.astype(jnp.bfloat16)
        d_qraw = (d_qlow * scale).astype(jnp.bfloat16)
        grad_scale = (
            jnp.sum(d_qlow * q_raw, axis=0)
            * jax.nn.sigmoid(scale_param)
            * (SOFT_BASE / math.sqrt(head_size))
        )
        grad_query = weight_outer(h_attn, d_qraw)
        grad_key = weight_outer(h_attn, keys_low)
        grad_value = weight_outer(h_attn, values_low)
        d_hattn = (
            times_transpose(d_qraw, back_query)
            + times_transpose(keys_low, back_key)
            + times_transpose(values_low, back_value)
        )
        d_norm_attn, grad_gain_attn = norm_back(d_hattn, normed_attn, inv_attn, gain_attn)
        in_grads.append(d_resid + d_norm_attn)
        grad_part = (
            grad_query,
            grad_key,
            grad_value,
            grad_out,
            grad_up,
            grad_down,
            grad_gain_attn,
            grad_gain_mlp,
            grad_scale,
        )
        if totals is None:
            totals = tuple(grad_part)
        else:
            totals = tuple((earlier + later for earlier, later in zip(totals, grad_part)))
    totals = (
        lax.psum_scatter(totals[0], ("dp", "seq"), scatter_dimension=0, tiled=True),
        lax.psum_scatter(totals[1], ("dp", "seq"), scatter_dimension=0, tiled=True),
        lax.psum_scatter(totals[2], ("dp", "seq"), scatter_dimension=0, tiled=True),
        lax.psum_scatter(totals[3], ("dp", "seq"), scatter_dimension=0, tiled=True),
        lax.psum_scatter(totals[4], ("dp", "seq"), scatter_dimension=0, tiled=True),
        lax.psum_scatter(totals[5], ("dp", "seq"), scatter_dimension=0, tiled=True),
        lax.psum_scatter(totals[6], ("dp", "seq"), scatter_dimension=0, tiled=True),
        lax.psum_scatter(totals[7], ("dp", "seq"), scatter_dimension=0, tiled=True),
        lax.psum_scatter(totals[8], ("dp", "seq"), scatter_dimension=0, tiled=True),
    )
    return (
        jnp.stack(results),
        jnp.stack(in_grads),
        totals[0],
        totals[1],
        totals[2],
        totals[3],
        totals[4],
        totals[5],
        totals[6],
        totals[7],
        totals[8],
    )


def solution(mesh):
    placed = (
        P("dp", "seq", None),
        P("dp", "seq", None),
        P(("dp", "seq"), None),
        P(("dp", "seq"), None),
        P(("dp", "seq"), None),
        P(("dp", "seq"), None),
        P(("dp", "seq"), None),
        P(("dp", "seq"), None),
        P(("dp", "seq")),
        P(("dp", "seq")),
        P(("dp", "seq")),
    )
    return jax.shard_map(
        per_device,
        mesh=mesh,
        in_specs=placed,
        out_specs=(
            P("dp", "seq", None),
            P("dp", "seq", None),
            P(("dp", "seq"), None),
            P(("dp", "seq"), None),
            P(("dp", "seq"), None),
            P(("dp", "seq"), None),
            P(("dp", "seq"), None),
            P(("dp", "seq"), None),
            P(("dp", "seq")),
            P(("dp", "seq")),
            P(("dp", "seq")),
        ),
        check_vma=False,
    )
```

profile of v0, /device:TPU:0, one launch (start us, length us, event | category | flops | bytes accessed | tf_op | source)
XLA Modules:
  0.0 1553.3 jit_solution(6274619430469553487)
XLA Ops:
  12.0 42.2 %all-reduce.7 = (bf16[1280]{0:T(1024)(128)(2,1)S(1)}, bf16[1280]{0:T(1024)(128)(2,1)S(1)}, bf16[1280]{0:T(1024)(128)(2,1)S(1)}) all-reduce(bf16[1280]{0:T(1024)(128)(2,1)S(1)} %dynamic-update-slice, bf16[1280]{0:T(1024)(128)(2,1)S(1)} %dynamic-update-slice.1, ...), channel_id=1, replica_groups=mesh['dp'=4,'seq'=8] {'dp','seq'}, use_global_device_ids=true, to_apply=%add | all-reduce | flops 3840 | bytes 15360
  55.5 17.4 %all-gather.15.cloned.1.call-done = bf16[1280,1280]{1,0:T(8,128)(2,1)} async-done(((bf16[40,1280]{1,0:T(8,128)(2,1)}), bf16[1280,1280]{1,0:T(8,128)(2,1)}) %all-gather.15.cloned.1.call-update) | async-done | bytes 3276816 | tf_op jit(solution)/shard_map/all_gather | solution.py:172
  76.5 57.7 %all-gather.21.cloned.1.call-done = bf16[1280,1280]{1,0:T(8,128)(2,1)} async-done(((bf16[40,1280]{1,0:T(8,128)(2,1)}), bf16[1280,1280]{1,0:T(8,128)(2,1)}) %all-gather.21.cloned.1.call-update) | async-done | bytes 3276816 | tf_op jit(solution)/shard_map/all_gather | solution.py:173
  146.4 48.9 %all-gather.19.cloned.1.call-done = bf16[1280,1280]{1,0:T(8,128)(2,1)} async-done(((bf16[40,1280]{1,0:T(8,128)(2,1)}), bf16[1280,1280]{1,0:T(8,128)(2,1)}) %all-gather.19.cloned.1.call-update) | async-done | bytes 3276816 | tf_op jit(solution)/shard_map/all_gather | solution.py:171
  203.1 26.5 %all-gather.31.cloned.1.call-done = bf16[1024,1280]{1,0:T(8,128)(2,1)} async-done(((bf16[128,1280]{1,0:T(8,128)(2,1)}), bf16[1024,1280]{1,0:T(8,128)(2,1)}) %all-gather.31.cloned.1.call-update) | async-done | bytes 2621456 | tf_op jit(solution)/shard_map/all_gather | solution.py:40
  229.6 34.4 %all-gather.33.cloned.1.call-done = bf16[1024,1280]{1,0:T(8,128)(2,1)} async-done(((bf16[128,1280]{1,0:T(8,128)(2,1)}), bf16[1024,1280]{1,0:T(8,128)(2,1)}) %all-gather.33.cloned.1.call-update) | async-done | bytes 2621456 | tf_op jit(solution)/shard_map/all_gather | solution.py:41
  264.0 18.8 %conditional.7 = (f32[16,128]{1,0:T(8,128)S(1)}, f32[16,128]{1,0:T(8,128)S(1)}, f32[16,128]{1,0:T(8,128)S(1)}, f32[128,1280]{1,0:T(8,128)S(1)}) conditional(s32[]{:T(128)} %convert_element_type.190, (s32[128]{0:T(128)S(1)}, bf16[1024,1280]{1,0:T(8,128)(2,1)}, bf16[128,16,80]{0,2,1:T(8,128)(2,1)}, bf16[1024,1280]{1,0:T(8,128)(2,1)}) %tuple.181, () %tuple.67), branch_computations={%region_7.10_spmd, %region_10.11_spmd} | conditional | flops 692357120 | bytes 87835224 | solution.py:67
  284.8 13.0 all-gather.17.cloned.1.call-done
  297.8 35.1 %all-gather.23.cloned.1.call-done = bf16[1024,1280]{1,0:T(8,128)(2,1)} async-done(((bf16[128,1280]{1,0:T(8,128)(2,1)}), bf16[1024,1280]{1,0:T(8,128)(2,1)}) %all-gather.23.cloned.1.call-update) | async-done | bytes 2621456 | tf_op jit(solution)/shard_map/all_gather | solution.py:41
  332.9 18.8 %conditional.6 = (f32[16,128]{1,0:T(8,128)S(1)}, f32[16,128]{1,0:T(8,128)S(1)}, f32[16,128]{1,0:T(8,128)S(1)}, f32[128,1280]{1,0:T(8,128)S(1)}) conditional(s32[]{:T(128)} %convert_element_type.190, (s32[128]{0:T(128)S(1)}, bf16[1024,1280]{1,0:T(8,128)(2,1)}, bf16[128,16,80]{0,2,1:T(8,128)(2,1)}, bf16[1024,1280]{1,0:T(8,128)(2,1)}) %tuple.179, () %tuple.65), branch_computations={%region_1.4_spmd, %region_4.5_spmd} | conditional | flops 692357120 | bytes 87835224 | solution.py:67
  355.7 38.4 %all-gather.25.cloned.1.call-done = bf16[1280,1280]{1,0:T(8,128)(2,1)} async-done(((bf16[40,1280]{1,0:T(8,128)(2,1)}), bf16[1280,1280]{1,0:T(8,128)(2,1)}) %all-gather.25.cloned.1.call-update) | async-done | bytes 3276816 | tf_op jit(solution)/shard_map/all_gather | solution.py:174
  397.8 57.5 %all-gather.27.cloned.1.call-done = bf16[1280,1280]{1,0:T(8,128)(2,1)} async-done(((bf16[40,1280]{1,0:T(8,128)(2,1)}), bf16[1280,1280]{1,0:T(8,128)(2,1)}) %all-gather.27.cloned.1.call-update) | async-done | bytes 3276816 | tf_op jit(solution)/shard_map/all_gather | solution.py:175
  458.7 57.6 %all-gather.29.cloned.1.call-done = bf16[1280,1280]{1,0:T(8,128)(2,1)} async-done(((bf16[40,1280]{1,0:T(8,128)(2,1)}), bf16[1280,1280]{1,0:T(8,128)(2,1)}) %all-gather.29.cloned.1.call-update) | async-done | bytes 3276816 | tf_op jit(solution)/shard_map/all_gather | solution.py:176
  542.6 26.9 %conditional.10 = (f32[128,1280]{1,0:T(8,128)S(1)}) conditional(s32[]{:T(128)} %convert_element_type.190, (s32[128]{0:T(128)S(1)}, bf16[1024,1280]{1,0:T(8,128)(2,1)}, bf16[128,16,80]{0,2,1:T(8,128)(2,1)S(1)}, f32[16,128]{1,0:T(8,128)S(1)}, bf16[128,1280]{1,0:T(8,128)(2,1)S(1)}, /*index=5*/bf16[1024,1280]{1,0:T(8,128)(2,1)}, ...), branch_computations={%region_21.22_spmd, %region_22.23_spmd} | conditional | flops 1017249792 | bytes 38683144 | solution.py:101
  558.5 9.6 fusion.53
  569.5 29.7 %conditional.8 = (f32[128,1280]{1,0:T(8,128)}) conditional(s32[]{:T(128)} %convert_element_type.190, (s32[128]{0:T(128)S(1)}, bf16[1024,1280]{1,0:T(8,128)(2,1)}, bf16[128,16,80]{0,2,1:T(8,128)(2,1)}, f32[16,128]{1,0:T(8,128)S(1)}, bf16[128,1280]{1,0:T(8,128)(2,1)}, /*index=5*/bf16[1024,1280]{1,0:T(8,128)(2,1)}, ...), branch_computations={%region_14.15_spmd, %region_15.16_spmd} | conditional | flops 1017249792 | bytes 38683144 | solution.py:101
  587.4 9.6 fusion.32
  624.6 15.4 all_gather.106
  640.0 15.1 all_gather.108
  655.0 13.9 all_gather.102
  669.0 14.8 all_gather.104
  683.8 35.7 %conditional.11 = (bf16[128,1280]{0,1:T(8,128)(2,1)}, bf16[128,1280]{0,1:T(8,128)(2,1)}) conditional(s32[]{:T(128)} %convert_element_type.218, (s32[128]{0:T(128)S(1)}, bf16[1024,1280]{1,0:T(8,128)(2,1)}, bf16[128,1280]{1,0:T(8,128)(2,1)}, f32[16,1024]{1,0:T(8,128)}, bf16[1024,1280]{1,0:T(8,128)(2,1)}, /*index=5*/bf16[128,1280]{1,0:T(8,128)(2,1)}, ...), branch_computations={%region_23.24_spmd, %region_24.25_spmd} | conditional | flops 1359413248 | bytes 49349136 | solution.py:144
  703.2 9.9 fusion.68
  719.5 32.6 %conditional.9 = (bf16[128,1280]{0,1:T(8,128)(2,1)S(1)}, bf16[128,1280]{0,1:T(8,128)(2,1)S(1)}) conditional(s32[]{:T(128)} %convert_element_type.218, (s32[128]{0:T(128)S(1)}, bf16[1024,1280]{1,0:T(8,128)(2,1)}, bf16[128,1280]{1,0:T(8,128)(2,1)S(1)}, f32[16,1024]{1,0:T(8,128)S(1)}, bf16[1024,1280]{1,0:T(8,128)(2,1)}, ...), branch_computations={%region_16.17_spmd, %region_17.18_spmd} | conditional | flops 1359413248 | bytes 49349136 | solution.py:144
  724.9 6.5 fusion.157
  737.0 9.2 fusion.47
  783.4 39.6 %all-reduce.6 = (f32[1280]{0:T(1024)S(1)}, f32[1280]{0:T(1024)S(1)}, f32[1280]{0:T(1024)S(1)}) all-reduce(f32[1280]{0:T(1024)S(1)} %add.209, f32[1280]{0:T(1024)S(1)} %add.210, f32[1280]{0:T(1024)S(1)} %fusion.131), channel_id=8, replica_groups=mesh['dp'=4,'seq'=8] {'dp','seq'}, use_global_device_ids=true, to_apply=%region_34.35.clone | all-reduce | flops 3840 | bytes 30720
  827.4 125.9 %reduce-scatter.13.cloned.1.call-done = f32[40,1280]{1,0:T(8,128)} async-done(((f32[1280,1280]{1,0:T(8,128)}), f32[40,1280]{1,0:T(8,128)}) %reduce-scatter.13.cloned.1.call-update) | async-done | bytes 204816 | tf_op jit(solution)/shard_map/reduce_scatter | solution.py:276
  953.3 147.9 %reduce-scatter.15.cloned.1.call-done = f32[40,1280]{1,0:T(8,128)} async-done(((f32[1280,1280]{1,0:T(8,128)}), f32[40,1280]{1,0:T(8,128)}) %reduce-scatter.15.cloned.1.call-update) | async-done | bytes 204816 | tf_op jit(solution)/shard_map/reduce_scatter | solution.py:277
  1101.2 147.9 %reduce-scatter.17.cloned.1.call-done = f32[40,1280]{1,0:T(8,128)} async-done(((f32[1280,1280]{1,0:T(8,128)}), f32[40,1280]{1,0:T(8,128)}) %reduce-scatter.17.cloned.1.call-update) | async-done | bytes 204816 | tf_op jit(solution)/shard_map/reduce_scatter | solution.py:278
  1249.1 148.5 %reduce-scatter.9.cloned.1.call-done = f32[40,1280]{1,0:T(8,128)} async-done(((f32[1280,1280]{1,0:T(8,128)}), f32[40,1280]{1,0:T(8,128)}) %reduce-scatter.9.cloned.1.call-update) | async-done | bytes 204816 | tf_op jit(solution)/shard_map/reduce_scatter | solution.py:274
  1397.6 148.6 %reduce-scatter.11.cloned.1.call-done = f32[40,1280]{1,0:T(8,128)} async-done(((f32[1280,1280]{1,0:T(8,128)}), f32[40,1280]{1,0:T(8,128)}) %reduce-scatter.11.cloned.1.call-update) | async-done | bytes 204816 | tf_op jit(solution)/shard_map/reduce_scatter | solution.py:275
  (256 shorter events, 246.6 us)
Async XLA Ops:
  7.2 127.0 %copy-start = (bf16[2,128,1280]{2,1,0:T(8,128)(2,1)S(1)}, bf16[2,128,1280]{2,1,0:T(8,128)(2,1)}, u32[]{:S(2)}) copy-start(bf16[2,128,1280]{2,1,0:T(8,128)(2,1)} %param.23) | copy-start | bytes 1966084
  7.2 65.8 %all-gather.15.cloned.1.call-start = ((), (), s32[]{:S(2)}) async-start(), calls=%async_computation.6 | async-start | bytes 3379200 | tf_op jit(solution)/shard_map/all_gather | solution.py:172
  7.9 126.2 %all-gather.21.cloned.1.call-start = ((), (), s32[]{:S(2)}) async-start(), calls=%async_computation.9 | async-start | bytes 3379200 | tf_op jit(solution)/shard_map/all_gather | solution.py:173
  8.7 186.6 %all-gather.19.cloned.1.call-start = ((), (), s32[]{:S(2)}) async-start(), calls=%async_computation.8 | async-start | bytes 3379200 | tf_op jit(solution)/shard_map/all_gather | solution.py:171
  9.4 220.2 %all-gather.31.cloned.1.call-start = ((), (), s32[]{:S(2)}) async-start(), calls=%async_computation.14 | async-start | bytes 2949120 | tf_op jit(solution)/shard_map/all_gather | solution.py:40
  54.2 92.1 %copy-start.40 = (bf16[1280]{0:T(1024)(128)(2,1)}, bf16[1280]{0:T(1024)(128)(2,1)S(1)}, u32[]{:S(2)}) copy-start(bf16[1280]{0:T(1024)(128)(2,1)S(1)} %get-tuple-element.289) | copy-start | bytes 7684
  76.4 187.6 %all-gather.33.cloned.1.call-start = ((), (), s32[]{:S(2)}) async-start(), calls=%async_computation.15 | async-start | bytes 2949120 | tf_op jit(solution)/shard_map/all_gather | solution.py:41
  137.5 160.3 %all-gather.17.cloned.1.call-start = ((), (), s32[]{:S(2)}) async-start(), calls=%async_computation.7 | async-start | bytes 2949120 | tf_op jit(solution)/shard_map/all_gather | solution.py:40
  140.9 192.1 %all-gather.23.cloned.1.call-start = ((), (), s32[]{:S(2)}) async-start(), calls=%async_computation.10 | async-start | bytes 2949120 | tf_op jit(solution)/shard_map/all_gather | solution.py:41
  144.2 250.0 %all-gather.25.cloned.1.call-start = ((), (), s32[]{:S(2)}) async-start(), calls=%async_computation.11 | async-start | bytes 3379200 | tf_op jit(solution)/shard_map/all_gather | solution.py:174
  145.0 310.4 %all-gather.27.cloned.1.call-start = ((), (), s32[]{:S(2)}) async-start(), calls=%async_computation.12 | async-start | bytes 3379200 | tf_op jit(solution)/shard_map/all_gather | solution.py:175
  145.7 370.6 %all-gather.29.cloned.1.call-start = ((), (), s32[]{:S(2)}) async-start(), calls=%async_computation.13 | async-start | bytes 3379200 | tf_op jit(solution)/shard_map/all_gather | solution.py:176
  146.3 537.5 %all-gather.39.cloned.1.call-start = ((), (), s32[]{:S(2)}) async-start(), calls=%async_computation.18 | async-start | bytes 2949120 | tf_op jit(solution)/shard_map/all_gather | solution.py:113
  199.8 64.2 %copy-start.26 = (bf16[128,1280]{1,0:T(8,128)(2,1)}, bf16[128,1280]{1,0:T(8,128)(2,1)S(1)}, u32[]{:S(2)}) copy-start(bf16[128,1280]{1,0:T(8,128)(2,1)S(1)} %get-tuple-element.305) | copy-start | bytes 983044
  199.8 484.0 %all-gather.41.cloned.1.call-start = ((), (), s32[]{:S(2)}) async-start(), calls=%async_computation.19 | async-start | bytes 2949120 | tf_op jit(solution)/shard_map/all_gather | solution.py:114
  269.6 3.8 copy-start.8
  354.3 173.0 %copy-start.10 = (f32[128,1280]{1,0:T(8,128)}, f32[128,1280]{1,0:T(8,128)S(1)}, u32[]{:S(2)}) copy-start(f32[128,1280]{1,0:T(8,128)S(1)} %div.48) | copy-start | bytes 1966084
  530.6 188.9 %all-gather.35.cloned.1.call-start = ((), (), s32[]{:S(2)}) async-start(), calls=%async_computation.16 | async-start | bytes 2949120 | tf_op jit(solution)/shard_map/all_gather | solution.py:113
  531.3 188.2 %all-gather.37.cloned.1.call-start = ((), (), s32[]{:S(2)}) async-start(), calls=%async_computation.17 | async-start | bytes 2949120 | tf_op jit(solution)/shard_map/all_gather | solution.py:114
  535.8 6.8 copy-start.23
  535.8 6.8 copy-start.27
  535.8 291.6 %reduce-scatter.7.cloned.1.call-start = ((), (), s32[]{:S(2)}) async-start(), calls=%async_computation.20 | async-start | bytes 6758400 | tf_op jit(solution)/shard_map/reduce_scatter | solution.py:273
  605.2 348.0 %reduce-scatter.13.cloned.1.call-start = ((), (), s32[]{:S(2)}) async-start(), calls=%async_computation.23 | async-start | bytes 6758400 | tf_op jit(solution)/shard_map/reduce_scatter | solution.py:276
  611.4 489.8 %reduce-scatter.15.cloned.1.call-start = ((), (), s32[]{:S(2)}) async-start(), calls=%async_computation.24 | async-start | bytes 6758400 | tf_op jit(solution)/shard_map/reduce_scatter | solution.py:277
  617.4 631.8 %reduce-scatter.17.cloned.1.call-start = ((), (), s32[]{:S(2)}) async-start(), calls=%async_computation.25 | async-start | bytes 6758400 | tf_op jit(solution)/shard_map/reduce_scatter | solution.py:278
  624.5 773.1 %reduce-scatter.9.cloned.1.call-start = ((), (), s32[]{:S(2)}) async-start(), calls=%async_computation.21 | async-start | bytes 6758400 | tf_op jit(solution)/shard_map/reduce_scatter | solution.py:274
  683.8 35.7 %copy-start.24 = (bf16[128,1280]{1,0:T(8,128)(2,1)S(1)}, bf16[128,1280]{1,0:T(8,128)(2,1)}, u32[]{:S(2)}) copy-start(bf16[128,1280]{1,0:T(8,128)(2,1)} %convolution_convert_fusion.5) | copy-start | bytes 983044
  683.8 35.7 %copy-start.25 = (bf16[128,1280]{1,0:T(8,128)(2,1)S(1)}, bf16[128,1280]{1,0:T(8,128)(2,1)}, u32[]{:S(2)}) copy-start(bf16[128,1280]{1,0:T(8,128)(2,1)} %convolution_convert_fusion.4) | copy-start | bytes 983044
  752.2 6.1 copy-start.34
  758.2 788.1 %reduce-scatter.11.cloned.1.call-start = ((), (), s32[]{:S(2)}) async-start(), calls=%async_computation.22 | async-start | bytes 6758400 | tf_op jit(solution)/shard_map/reduce_scatter | solution.py:275
  781.1 43.6 %copy-start.15 = (f32[128,1280]{1,0:T(8,128)S(1)}, f32[128,1280]{1,0:T(8,128)}, u32[]{:S(2)}) copy-start(f32[128,1280]{1,0:T(8,128)} %copy-done.13) | copy-start | bytes 1966084
  781.1 43.6 %copy-start.18 = (f32[128,1280]{1,0:T(8,128)S(1)}, f32[128,1280]{1,0:T(8,128)}, u32[]{:S(2)}) copy-start(f32[128,1280]{1,0:T(8,128)} %get-tuple-element.301) | copy-start | bytes 1966084
  (32 other events, 71.4 us)
Sparse Core Ops, SparseCore 0:
  10.9 62.0 all-gather.14
  75.8 58.2 all-gather.20
  137.0 58.2 all-gather.18
  196.8 32.7 all-gather.30
  231.1 32.8 all-gather.32
  265.5 32.2 all-gather.16
  299.4 33.4 all-gather.22
  335.8 58.3 all-gather.24
  397.0 58.2 all-gather.26
  458.0 58.2 all-gather.28
  518.0 32.7 all-gather.38
  552.3 32.8 all-gather.40
  586.8 32.8 all-gather.34
  621.2 33.7 all-gather.36
  657.7 147.1 reduce-scatter.6
  807.7 145.5 reduce-scatter.12
  956.0 145.1 reduce-scatter.14
  1103.9 145.1 reduce-scatter.16
  1252.0 145.5 reduce-scatter.8
  1400.3 145.8 reduce-scatter.10
where the time goes:
time: 1560 us; the launch traced here: 1550 us
  waiting for transfers between devices  1110 us (71%)
  matrix products  182 us (12%)
  blocking collectives  141 us (9%)
  local copies, waits for them, and re-layouts  84 us (5%)
  other arithmetic  19.1 us (1%)
    reduce_scatter x1, waiting for transfers between devices, per_device(): lax.psum_scatter(totals[2], ('dp', 'seq'), scatter_dimension=0, tiled=True)  149 us
    reduce_scatter x1, waiting for transfers between devices, per_device(): lax.psum_scatter(totals[1], ('dp', 'seq'), scatter_dimension=0, tiled=True)  148 us
    reduce_scatter x1, waiting for transfers between devices, per_device(): lax.psum_scatter(totals[5], ('dp', 'seq'), scatter_dimension=0, tiled=True)  148 us
    reduce_scatter x1, waiting for transfers between devices, per_device(): lax.psum_scatter(totals[4], ('dp', 'seq'), scatter_dimension=0, tiled=True)  148 us
    reduce_scatter x1, waiting for transfers between devices, per_device(): lax.psum_scatter(totals[3], ('dp', 'seq'), scatter_dimension=0, tiled=True)  126 us
    unnamed x2, blocking collectives  81.8 us
    all_gather x2, waiting for transfers between devices, attend(): value_piece = lax.all_gather(v_low, 'seq', axis=0, tiled=True)  69.5 us
    all_gather x1, waiting for transfers between devices, per_device(): lax.all_gather(w_value, ('dp', 'seq'), axis=0, tiled=True)  57.7 us
  transfers between devices with their start and end apart: 20, of which 15 were waited for; matrix products, arithmetic and copies ran while one was open for 18% of the time, Pallas kernels for 0%

commit v1 on v0

--- a/solution.py
+++ b/solution.py
@@ -37,7 +37,15 @@
         jnp.zeros((num_heads, group_rows), jnp.float32),
         jnp.zeros((group_rows, model_width), jnp.float32),
     )
-    key_piece = lax.all_gather(k_low, "seq", axis=0, tiled=True)
+    ways, here = (lax.axis_size("seq"), lax.axis_index("seq"))
+    grown, reach = (k_low, 1)
+    while reach < ways:
+        theirs = lax.ppermute(grown, "seq", [(d, d ^ reach) for d in range(ways)])
+        mine_first = jnp.concatenate([grown, theirs], axis=0)
+        theirs_first = jnp.concatenate([theirs, grown], axis=0)
+        grown = jnp.where(here & reach == 0, mine_first, theirs_first)
+        reach = 2 * reach
+    key_piece = grown
     value_piece = lax.all_gather(v_low, "seq", axis=0, tiled=True)
     count = key_piece.shape[0]
 

time: 1560 us -> 1630 us (1.045)
  waiting for transfers between devices: 1110 us -> 1150 us
    ppermute x0 -> x6, waiting for transfers between devices: none -> 104 us  [attend(): theirs = lax.ppermute(grown, 'seq', [(d, d ^ reach) for d in range(ways)])]
    all_gather x2, waiting for transfers between devices: 69.5 us -> 0.01 us  [attend(): value_piece = lax.all_gather(v_low, 'seq', axis=0, tiled=True)]
    all_gather x1, waiting for transfers between devices: 57.7 us -> 17.5 us  [per_device(): lax.all_gather(w_value, ('dp', 'seq'), axis=0, tiled=True)]
    all_gather x1, waiting for transfers between devices: 17.4 us -> 52.2 us  [per_device(): lax.all_gather(w_key, ('dp', 'seq'), axis=0, tiled=True)]
    reduce_scatter x1, waiting for transfers between devices: 0.01 us -> 33.3 us  [per_device(): lax.psum_scatter(totals[0], ('dp', 'seq'), scatter_dimension=0, tiled=True)]
    all_gather x1, waiting for transfers between devices: 38.4 us -> 14.6 us  [per_device(): lax.all_gather(w_out, ('dp', 'seq'), axis=0, tiled=True)]
    all_gather x2, waiting for transfers between devices: 39.5 us -> 15.7 us  [query_grads(): key_piece = lax.all_gather(k_low, 'seq', axis=0, tiled=True)]
    reduce_scatter x1, waiting for transfers between devices: 126 us -> 148 us  [per_device(): lax.psum_scatter(totals[3], ('dp', 'seq'), scatter_dimension=0, tiled=True)]
  transfers between devices with their start and end apart: 20 -> 26, of which waited for: 15 -> 19; matrix products, arithmetic and copies ran while one was open for 18% -> 18% of each run, Pallas kernels for 0% -> 0%
where the time goes in v1:
time: 1630 us; the launch traced here: 1620 us
  waiting for transfers between devices  1150 us (71%)
  matrix products  178 us (11%)
  blocking collectives  141 us (9%)
  local copies, waits for them, and re-layouts  97.2 us (6%)
  other arithmetic  31.2 us (2%)
    reduce_scatter x1, waiting for transfers between devices, per_device(): lax.psum_scatter(totals[1], ('dp', 'seq'), scatter_dimension=0, tiled=True)  148 us
    reduce_scatter x1, waiting for transfers between devices, per_device(): lax.psum_scatter(totals[5], ('dp', 'seq'), scatter_dimension=0, tiled=True)  148 us
    reduce_scatter x1, waiting for transfers between devices, per_device(): lax.psum_scatter(totals[3], ('dp', 'seq'), scatter_dimension=0, tiled=True)  148 us
    reduce_scatter x1, waiting for transfers between devices, per_device(): lax.psum_scatter(totals[4], ('dp', 'seq'), scatter_dimension=0, tiled=True)  148 us
    reduce_scatter x1, waiting for transfers between devices, per_device(): lax.psum_scatter(totals[2], ('dp', 'seq'), scatter_dimension=0, tiled=True)  148 us
    ppermute x6, waiting for transfers between devices, attend(): theirs = lax.ppermute(grown, 'seq', [(d, d ^ reach) for d in range(ways)])  104 us
    unnamed x2, blocking collectives  81.9 us
    another operation x20, local copies, waits for them, and re-layouts  62.8 us
  transfers between devices with their start and end apart: 26, of which 19 were waited for; matrix products, arithmetic and copies ran while one was open for 18% of the time, Pallas kernels for 0%

profile of v1, /device:TPU:0, one launch (start us, length us, event | category | flops | bytes accessed | tf_op | source)
XLA Modules:
  0.0 1623.5 jit_solution(17894942326029908592)
XLA Ops:
  12.0 42.2 %all-reduce.7 = (bf16[1280]{0:T(1024)(128)(2,1)S(1)}, bf16[1280]{0:T(1024)(128)(2,1)S(1)}, bf16[1280]{0:T(1024)(128)(2,1)S(1)}) all-reduce(bf16[1280]{0:T(1024)(128)(2,1)S(1)} %dynamic-update-slice, bf16[1280]{0:T(1024)(128)(2,1)S(1)} %dynamic-update-slice.1, ...), channel_id=1, replica_groups=mesh['dp'=4,'seq'=8] {'dp','seq'}, use_global_device_ids=true, to_apply=%add | all-reduce | flops 3840 | bytes 15360
  55.5 17.5 %all-gather.19.cloned.1.call-done = bf16[1280,1280]{1,0:T(8,128)(2,1)} async-done(((bf16[40,1280]{1,0:T(8,128)(2,1)}), bf16[1280,1280]{1,0:T(8,128)(2,1)}) %all-gather.19.cloned.1.call-update) | async-done | bytes 3276816 | tf_op jit(solution)/shard_map/all_gather | solution.py:181
  81.9 52.2 %all-gather.15.cloned.1.call-done = bf16[1280,1280]{1,0:T(8,128)(2,1)} async-done(((bf16[40,1280]{1,0:T(8,128)(2,1)}), bf16[1280,1280]{1,0:T(8,128)(2,1)}) %all-gather.15.cloned.1.call-update) | async-done | bytes 3276816 | tf_op jit(solution)/shard_map/all_gather | solution.py:180
  146.2 16.5 %collective-permute-done.4 = bf16[256,1280]{1,0:T(8,128)(2,1)} collective-permute-done((bf16[256,1280]{1,0:T(8,128)(2,1)S(1)}, bf16[256,1280]{1,0:T(8,128)(2,1)}, u32[]{:S(2)}, u32[]{:S(2)}) %collective-permute-start.4) | collective-permute-done | bytes 655392 | tf_op jit(solution)/shard_map/ppermute | solution.py:43
  165.3 27.3 %collective-permute-done.1 = bf16[256,1280]{1,0:T(8,128)(2,1)} collective-permute-done((bf16[256,1280]{1,0:T(8,128)(2,1)S(1)}, bf16[256,1280]{1,0:T(8,128)(2,1)}, u32[]{:S(2)}, u32[]{:S(2)}) %collective-permute-start.1) | collective-permute-done | bytes 655392 | tf_op jit(solution)/shard_map/ppermute | solution.py:43
  195.3 57.0 %all-gather.17.cloned.1.call-done = bf16[1280,1280]{1,0:T(8,128)(2,1)} async-done(((bf16[40,1280]{1,0:T(8,128)(2,1)}), bf16[1280,1280]{1,0:T(8,128)(2,1)}) %all-gather.17.cloned.1.call-update) | async-done | bytes 3276816 | tf_op jit(solution)/shard_map/all_gather | solution.py:179
  270.5 53.7 %collective-permute-done.2 = bf16[512,1280]{1,0:T(8,128)(2,1)} collective-permute-done((bf16[512,1280]{1,0:T(8,128)(2,1)S(1)}, bf16[512,1280]{1,0:T(8,128)(2,1)}, u32[]{:S(2)}, u32[]{:S(2)}) %collective-permute-start.2) | collective-permute-done | bytes 1310752 | tf_op jit(solution)/shard_map/ppermute | solution.py:43
  328.1 23.3 %conditional.7 = (f32[16,128]{1,0:T(8,128)S(1)}, f32[16,128]{1,0:T(8,128)S(1)}, f32[16,128]{1,0:T(8,128)S(1)}, f32[128,1280]{1,0:T(8,128)S(1)}) conditional(s32[]{:T(128)} %convert_element_type.190, (s32[128]{0:T(128)S(1)}, pred[]{:T(512)}, bf16[1024,1280]{1,0:T(8,128)(2,1)}, bf16[1024,1280]{1,0:T(8,128)(2,1)}, bf16[128,16,80]{0,2,1:T(8,128)(2,1)}, ...), branch_computations={%region_7.10_spmd, %region_10.11_spmd} | conditional | flops 693667840 | bytes 102253176 | solution.py:75
  353.4 23.5 %conditional.6 = (f32[16,128]{1,0:T(8,128)S(1)}, f32[16,128]{1,0:T(8,128)S(1)}, f32[16,128]{1,0:T(8,128)S(1)}, f32[128,1280]{1,0:T(8,128)S(1)}) conditional(s32[]{:T(128)} %convert_element_type.190, (s32[128]{0:T(128)S(1)}, pred[]{:T(512)}, bf16[1024,1280]{1,0:T(8,128)(2,1)}, bf16[1024,1280]{1,0:T(8,128)(2,1)}, bf16[128,16,80]{0,2,1:T(8,128)(2,1)}, ...), branch_computations={%region_1.4_spmd, %region_4.5_spmd} | conditional | flops 693667840 | bytes 102253176 | solution.py:75
  381.3 14.6 all-gather.23.cloned.1.call-done
  399.5 57.5 %all-gather.25.cloned.1.call-done = bf16[1280,1280]{1,0:T(8,128)(2,1)} async-done(((bf16[40,1280]{1,0:T(8,128)(2,1)}), bf16[1280,1280]{1,0:T(8,128)(2,1)}) %all-gather.25.cloned.1.call-update) | async-done | bytes 3276816 | tf_op jit(solution)/shard_map/all_gather | solution.py:183
  460.4 57.7 %all-gather.27.cloned.1.call-done = bf16[1280,1280]{1,0:T(8,128)(2,1)} async-done(((bf16[40,1280]{1,0:T(8,128)(2,1)}), bf16[1280,1280]{1,0:T(8,128)(2,1)}) %all-gather.27.cloned.1.call-update) | async-done | bytes 3276816 | tf_op jit(solution)/shard_map/all_gather | solution.py:184
  544.5 8.1 all-gather.37.cloned.1.call-done
  552.6 26.7 %conditional.10 = (f32[128,1280]{1,0:T(8,128)S(1)}) conditional(s32[]{:T(128)} %convert_element_type.190, (s32[128]{0:T(128)S(1)}, bf16[1024,1280]{1,0:T(8,128)(2,1)}, bf16[128,16,80]{0,2,1:T(8,128)(2,1)S(1)}, f32[16,128]{1,0:T(8,128)S(1)}, bf16[128,1280]{1,0:T(8,128)(2,1)S(1)}, /*index=5*/bf16[1024,1280]{1,0:T(8,128)(2,1)}, ...), branch_computations={%region_21.22_spmd, %region_22.23_spmd} | conditional | flops 1017249792 | bytes 38683144 | solution.py:109
  568.4 9.6 fusion.55
  587.0 29.7 %conditional.8 = (f32[128,1280]{1,0:T(8,128)}) conditional(s32[]{:T(128)} %convert_element_type.190, (s32[128]{0:T(128)S(1)}, bf16[1024,1280]{1,0:T(8,128)(2,1)}, bf16[128,16,80]{0,2,1:T(8,128)(2,1)}, f32[16,128]{1,0:T(8,128)S(1)}, bf16[128,1280]{1,0:T(8,128)(2,1)}, /*index=5*/bf16[1024,1280]{1,0:T(8,128)(2,1)}, ...), branch_computations={%region_14.15_spmd, %region_15.16_spmd} | conditional | flops 1017249792 | bytes 38683144 | solution.py:109
  604.8 9.8 fusion.34
  642.1 15.5 all_gather.104
  657.6 15.0 all_gather.106
  672.6 14.0 all_gather.99
  686.6 15.1 all_gather.101
  701.7 32.9 %conditional.11 = (bf16[128,1280]{0,1:T(8,128)(2,1)S(1)}, bf16[128,1280]{0,1:T(8,128)(2,1)}) conditional(s32[]{:T(128)} %convert_element_type.218, (s32[128]{0:T(128)S(1)}, bf16[1024,1280]{1,0:T(8,128)(2,1)}, bf16[128,1280]{1,0:T(8,128)(2,1)S(1)}, f32[16,1024]{1,0:T(8,128)}, bf16[1024,1280]{1,0:T(8,128)(2,1)}, ...), branch_computations={%region_23.24_spmd, %region_24.25_spmd} | conditional | flops 1359413248 | bytes 50659884 | solution.py:152
  719.1 9.2 fusion.70
  734.7 32.7 %conditional.9 = (bf16[128,1280]{0,1:T(8,128)(2,1)S(1)}, bf16[128,1280]{0,1:T(8,128)(2,1)S(1)}) conditional(s32[]{:T(128)} %convert_element_type.218, (s32[128]{0:T(128)S(1)}, bf16[1024,1280]{1,0:T(8,128)(2,1)}, bf16[128,1280]{1,0:T(8,128)(2,1)S(1)}, f32[16,1024]{1,0:T(8,128)S(1)}, bf16[1024,1280]{1,0:T(8,128)(2,1)}, ...), branch_computations={%region_16.17_spmd, %region_17.18_spmd} | conditional | flops 1359413248 | bytes 50659884 | solution.py:152
  752.1 9.3 fusion.49
  798.9 39.7 %all-reduce.6 = (f32[1280]{0:T(1024)S(1)}, f32[1280]{0:T(1024)S(1)}, f32[1280]{0:T(1024)S(1)}) all-reduce(f32[1280]{0:T(1024)S(1)} %add.209, f32[1280]{0:T(1024)S(1)} %add.210, f32[1280]{0:T(1024)S(1)} %fusion.133), channel_id=8, replica_groups=mesh['dp'=4,'seq'=8] {'dp','seq'}, use_global_device_ids=true, to_apply=%region_34.35.clone | all-reduce | flops 3840 | bytes 30720
  842.9 33.3 %reduce-scatter.7.cloned.1.call-done = f32[40,1280]{1,0:T(8,128)} async-done(((f32[1280,1280]{1,0:T(8,128)}), f32[40,1280]{1,0:T(8,128)}) %reduce-scatter.7.cloned.1.call-update) | async-done | bytes 204816 | tf_op jit(solution)/shard_map/reduce_scatter | solution.py:281
  876.2 148.2 %reduce-scatter.13.cloned.1.call-done = f32[40,1280]{1,0:T(8,128)} async-done(((f32[1280,1280]{1,0:T(8,128)}), f32[40,1280]{1,0:T(8,128)}) %reduce-scatter.13.cloned.1.call-update) | async-done | bytes 204816 | tf_op jit(solution)/shard_map/reduce_scatter | solution.py:284
  1024.4 147.7 %reduce-scatter.15.cloned.1.call-done = f32[40,1280]{1,0:T(8,128)} async-done(((f32[1280,1280]{1,0:T(8,128)}), f32[40,1280]{1,0:T(8,128)}) %reduce-scatter.15.cloned.1.call-update) | async-done | bytes 204816 | tf_op jit(solution)/shard_map/reduce_scatter | solution.py:285
  1172.1 148.2 %reduce-scatter.17.cloned.1.call-done = f32[40,1280]{1,0:T(8,128)} async-done(((f32[1280,1280]{1,0:T(8,128)}), f32[40,1280]{1,0:T(8,128)}) %reduce-scatter.17.cloned.1.call-update) | async-done | bytes 204816 | tf_op jit(solution)/shard_map/reduce_scatter | solution.py:286
  1320.3 148.5 %reduce-scatter.9.cloned.1.call-done = f32[40,1280]{1,0:T(8,128)} async-done(((f32[1280,1280]{1,0:T(8,128)}), f32[40,1280]{1,0:T(8,128)}) %reduce-scatter.9.cloned.1.call-update) | async-done | bytes 204816 | tf_op jit(solution)/shard_map/reduce_scatter | solution.py:282
  1468.8 147.6 %reduce-scatter.11.cloned.1.call-done = f32[40,1280]{1,0:T(8,128)} async-done(((f32[1280,1280]{1,0:T(8,128)}), f32[40,1280]{1,0:T(8,128)}) %reduce-scatter.11.cloned.1.call-update) | async-done | bytes 204816 | tf_op jit(solution)/shard_map/reduce_scatter | solution.py:283
  (294 shorter events, 293.2 us)
Async XLA Ops:
  7.2 69.3 %copy-start = (bf16[2,128,1280]{2,1,0:T(8,128)(2,1)S(1)}, bf16[2,128,1280]{2,1,0:T(8,128)(2,1)}, u32[]{:S(2)}) copy-start(bf16[2,128,1280]{2,1,0:T(8,128)(2,1)} %param.23) | copy-start | bytes 1966084
  7.2 65.8 %all-gather.19.cloned.1.call-start = ((), (), s32[]{:S(2)}) async-start(), calls=%async_computation.8 | async-start | bytes 3379200 | tf_op jit(solution)/shard_map/all_gather | solution.py:181
  7.9 126.2 %all-gather.15.cloned.1.call-start = ((), (), s32[]{:S(2)}) async-start(), calls=%async_computation.6 | async-start | bytes 3379200 | tf_op jit(solution)/shard_map/all_gather | solution.py:180
  8.7 243.6 %all-gather.17.cloned.1.call-start = ((), (), s32[]{:S(2)}) async-start(), calls=%async_computation.7 | async-start | bytes 3379200 | tf_op jit(solution)/shard_map/all_gather | solution.py:179
  9.4 318.7 %all-gather.29.cloned.1.call-start = ((), (), s32[]{:S(2)}) async-start(), calls=%async_computation.13 | async-start | bytes 2949120 | tf_op jit(solution)/shard_map/all_gather | solution.py:49
  54.2 141.1 %copy-start.48 = (bf16[1280]{0:T(1024)(128)(2,1)}, bf16[1280]{0:T(1024)(128)(2,1)S(1)}, u32[]{:S(2)}) copy-start(bf16[1280]{0:T(1024)(128)(2,1)S(1)} %get-tuple-element.317) | copy-start | bytes 7684
  76.4 277.0 %all-gather.21.cloned.1.call-start = ((), (), s32[]{:S(2)}) async-start(), calls=%async_computation.9 | async-start | bytes 2949120 | tf_op jit(solution)/shard_map/all_gather | solution.py:49
  79.8 316.1 %all-gather.23.cloned.1.call-start = ((), (), s32[]{:S(2)}) async-start(), calls=%async_computation.10 | async-start | bytes 3379200 | tf_op jit(solution)/shard_map/all_gather | solution.py:182
  80.4 376.6 %all-gather.25.cloned.1.call-start = ((), (), s32[]{:S(2)}) async-start(), calls=%async_computation.11 | async-start | bytes 3379200 | tf_op jit(solution)/shard_map/all_gather | solution.py:183
  81.1 437.0 %all-gather.27.cloned.1.call-start = ((), (), s32[]{:S(2)}) async-start(), calls=%async_computation.12 | async-start | bytes 3379200 | tf_op jit(solution)/shard_map/all_gather | solution.py:184
  81.9 470.7 %all-gather.37.cloned.1.call-start = ((), (), s32[]{:S(2)}) async-start(), calls=%async_computation.17 | async-start | bytes 2949120 | tf_op jit(solution)/shard_map/all_gather | solution.py:89
  137.5 449.5 %all-gather.31.cloned.1.call-start = ((), (), s32[]{:S(2)}) async-start(), calls=%async_computation.14 | async-start | bytes 2949120 | tf_op jit(solution)/shard_map/all_gather | solution.py:89
  140.9 560.8 %all-gather.39.cloned.1.call-start = ((), (), s32[]{:S(2)}) async-start(), calls=%async_computation.18 | async-start | bytes 2949120 | tf_op jit(solution)/shard_map/all_gather | solution.py:121
  140.9 1.7 collective-permute-start.3
  141.3 2.3 collective-permute-start
  142.8 19.9 %collective-permute-start.4 = (bf16[256,1280]{1,0:T(8,128)(2,1)S(1)}, bf16[256,1280]{1,0:T(8,128)(2,1)}, u32[]{:S(2)}, u32[]{:S(2)}) collective-permute-start(bf16[256,1280]{1,0:T(8,128)(2,1)S(1)} %maximum_select_fusion.3), channel_id=1, source_target_pairs={{0,2},{1,3},{2,0},{3,1},{4,6},{5,7},{6,4},{7,5},{8,10},{9,11},{10,... | collective-permute-start | bytes 1966088 | tf_op jit(solution)/shard_map/ppermute | solution.py:43
  144.9 47.8 %collective-permute-start.1 = (bf16[256,1280]{1,0:T(8,128)(2,1)S(1)}, bf16[256,1280]{1,0:T(8,128)(2,1)}, u32[]{:S(2)}, u32[]{:S(2)}) collective-permute-start(bf16[256,1280]{1,0:T(8,128)(2,1)S(1)} %maximum_select_fusion.2), channel_id=1, source_target_pairs={{0,2},{1,3},{2,0},{3,1},{4,6},{5,7},{6,4},{7,5},{8,10},{9,11},{10,... | collective-permute-start | bytes 1966088 | tf_op jit(solution)/shard_map/ppermute | solution.py:43
  164.3 102.3 %collective-permute-start.5 = (bf16[512,1280]{1,0:T(8,128)(2,1)S(1)}, bf16[512,1280]{1,0:T(8,128)(2,1)}, u32[]{:S(2)}, u32[]{:S(2)}) collective-permute-start(bf16[512,1280]{1,0:T(8,128)(2,1)S(1)} %maximum_select_fusion.1), channel_id=1, source_target_pairs={{0,4},{1,5},{2,6},{3,7},{4,0},{5,1},{6,2},{7,3},{8,12},{9,13},{10,... | collective-permute-start | bytes 3932168 | tf_op jit(solution)/shard_map/ppermute | solution.py:43
  194.6 129.6 %collective-permute-start.2 = (bf16[512,1280]{1,0:T(8,128)(2,1)S(1)}, bf16[512,1280]{1,0:T(8,128)(2,1)}, u32[]{:S(2)}, u32[]{:S(2)}) collective-permute-start(bf16[512,1280]{1,0:T(8,128)(2,1)S(1)} %maximum_select_fusion), channel_id=1, source_target_pairs={{0,4},{1,5},{2,6},{3,7},{4,0},{5,1},{6,2},{7,3},{8,12},{9,13},{10,... | collective-permute-start | bytes 3932168 | tf_op jit(solution)/shard_map/ppermute | solution.py:43
  260.7 441.0 %all-gather.41.cloned.1.call-start = ((), (), s32[]{:S(2)}) async-start(), calls=%async_computation.19 | async-start | bytes 2949120 | tf_op jit(solution)/shard_map/all_gather | solution.py:122
  379.9 149.3 %copy-start.10 = (f32[128,1280]{1,0:T(8,128)}, f32[128,1280]{1,0:T(8,128)S(1)}, u32[]{:S(2)}) copy-start(f32[128,1280]{1,0:T(8,128)S(1)} %div.48) | copy-start | bytes 1966084
  532.5 202.1 %all-gather.33.cloned.1.call-start = ((), (), s32[]{:S(2)}) async-start(), calls=%async_computation.15 | async-start | bytes 2949120 | tf_op jit(solution)/shard_map/all_gather | solution.py:121
  533.3 201.4 %all-gather.35.cloned.1.call-start = ((), (), s32[]{:S(2)}) async-start(), calls=%async_computation.16 | async-start | bytes 2949120 | tf_op jit(solution)/shard_map/all_gather | solution.py:122
  537.7 338.5 %reduce-scatter.7.cloned.1.call-start = ((), (), s32[]{:S(2)}) async-start(), calls=%async_computation.20 | async-start | bytes 6758400 | tf_op jit(solution)/shard_map/reduce_scatter | solution.py:281
  622.9 401.5 %reduce-scatter.13.cloned.1.call-start = ((), (), s32[]{:S(2)}) async-start(), calls=%async_computation.23 | async-start | bytes 6758400 | tf_op jit(solution)/shard_map/reduce_scatter | solution.py:284
  629.0 543.1 %reduce-scatter.15.cloned.1.call-start = ((), (), s32[]{:S(2)}) async-start(), calls=%async_computation.24 | async-start | bytes 6758400 | tf_op jit(solution)/shard_map/reduce_scatter | solution.py:285
  635.0 685.4 %reduce-scatter.17.cloned.1.call-start = ((), (), s32[]{:S(2)}) async-start(), calls=%async_computation.25 | async-start | bytes 6758400 | tf_op jit(solution)/shard_map/reduce_scatter | solution.py:286
  642.0 59.7 %copy-start.22 = (bf16[128,1280]{1,0:T(8,128)(2,1)S(1)}, bf16[128,1280]{1,0:T(8,128)(2,1)}, u32[]{:S(2)}) copy-start(bf16[128,1280]{1,0:T(8,128)(2,1)} %convolution_convert_fusion.3) | copy-start | bytes 983044
  642.0 826.8 %reduce-scatter.9.cloned.1.call-start = ((), (), s32[]{:S(2)}) async-start(), calls=%async_computation.21 | async-start | bytes 6758400 | tf_op jit(solution)/shard_map/reduce_scatter | solution.py:282
  773.1 843.3 %reduce-scatter.11.cloned.1.call-start = ((), (), s32[]{:S(2)}) async-start(), calls=%async_computation.22 | async-start | bytes 6758400 | tf_op jit(solution)/shard_map/reduce_scatter | solution.py:283
  796.6 43.7 %copy-start.15 = (f32[128,1280]{1,0:T(8,128)S(1)}, f32[128,1280]{1,0:T(8,128)}, u32[]{:S(2)}) copy-start(f32[128,1280]{1,0:T(8,128)} %copy-done.13) | copy-start | bytes 1966084
  796.6 43.7 %copy-start.18 = (f32[128,1280]{1,0:T(8,128)S(1)}, f32[128,1280]{1,0:T(8,128)}, u32[]{:S(2)}) copy-start(f32[128,1280]{1,0:T(8,128)} %get-tuple-element.333) | copy-start | bytes 1966084
  (46 other events, 211.2 us)
Sparse Core Ops, SparseCore 0:
  10.9 62.0 all-gather.18
  75.8 58.2 all-gather.14
  137.0 115.2 all-gather.16
  253.8 43.4 all-gather.28
  298.8 36.1 all-gather.20
  337.7 58.1 all-gather.22
  398.7 58.2 all-gather.24
  459.9 58.2 all-gather.26
  519.8 32.7 all-gather.36
  554.1 32.8 all-gather.30
  588.7 32.8 all-gather.38
  623.1 33.3 all-gather.40
  658.1 33.5 all-gather.32
  693.2 32.8 all-gather.34
  728.8 147.4 reduce-scatter.6
  879.0 145.3 reduce-scatter.12
  1027.1 144.8 reduce-scatter.14
  1174.8 145.4 reduce-scatter.16
  1323.2 145.5 reduce-scatter.8
  1471.5 144.8 reduce-scatter.10
